TPU v7x, 256 devices: a whole 4x4x8 slice. The times are simulated.
256 devices in a mesh: dp: 32 (over x, y, core), mp: 8 (over z).
Axes of the slice: x: 4, y: 4, z: 8, core: 2. Of those that a mesh axis runs over, the one named last changes fastest.
Arguments:
- features: bfloat16 [65536, 2, 512], P('dp'), may hold values from -27 to 27
- projection: bfloat16 [512, 256], replicated, may hold values from -1 to 1
- prototypes: float32 [3000, 256], P('mp'), may hold values from -7 to 7
Outputs:
- grad_prototypes: float32 [3000, 256], P('mp')
- grad_projection: float32 [512, 256], replicated
- loss: float32 [], replicated
All inputs are finite; a program needn't handle non-finite values.
Results may differ from a plain program's by a relative error of at most 0.0019.
The roundings to bfloat16 on the way count: a program that leaves them out, or rounds other values in their place, can miss the bound.
Values may be sent and summed in bfloat16 or wider, within the bound.
A program may use at most 128 MiB of HBM per device.

v0:
```python
import jax
import jax.numpy as jnp
from jax import lax
from jax.sharding import PartitionSpec as P

ITERS = 3
EPSILON_CODES = 0.05
SOFTMAX_TEMPER = 0.1
LOSS_FACTOR = 4096.0
TINY = 1e-06


def unit_rows(values):
    inverse = lax.rsqrt(jnp.sum(values * values, axis=-1, keepdims=True) + TINY)
    return (values * inverse, inverse)


def prototype_totals(values):
    return lax.psum(jnp.sum(values, axis=0), "dp")


def code_totals(values):
    return lax.psum(jnp.sum(values, axis=-1), "mp")


def loss_pieces(
    prototype_logits, softmax_exponent, softmax_denominator, assignments, gradient_factor
):
    swapped_targets = assignments[:, ::-1]
    grad_half = (
        (softmax_exponent / softmax_denominator[..., None] - swapped_targets) * gradient_factor
    ).astype(jnp.bfloat16)
    loss_portion = jnp.sum(
        swapped_targets
        * (prototype_logits * (1.0 / SOFTMAX_TEMPER) - jnp.log(softmax_denominator)[..., None])
    )
    return (grad_half, loss_portion)


def embed_backward(grad_unit, embed_unit, embed_inverse, own_feats):
    along_unit = jnp.sum(embed_unit * grad_unit, axis=-1, keepdims=True)
    grad_raw = ((grad_unit - embed_unit * along_unit) * embed_inverse).astype(jnp.bfloat16)
    return jnp.einsum("bve,bvp->ep", own_feats, grad_raw, preferred_element_type=jnp.float32)


def body(features, projection, prototypes):
    local_rows = features.shape[0]
    own_count = local_rows // lax.axis_size("mp")
    batch_row_count = local_rows * lax.axis_size("dp")
    gradient_factor = LOSS_FACTOR / (2.0 * batch_row_count * SOFTMAX_TEMPER)
    proto_unit, proto_inverse = unit_rows(prototypes)
    proto_half = proto_unit.astype(jnp.bfloat16)
    first_row = lax.axis_index("mp") * own_count
    own_feats = lax.dynamic_slice_in_dim(features, first_row, own_count, 0)
    raw_embed = jnp.einsum("bve,ep->bvp", own_feats, projection, preferred_element_type=jnp.float32)
    embed_unit, embed_inverse = unit_rows(raw_embed)
    embed_half = embed_unit.astype(jnp.bfloat16)
    all_embed = lax.all_gather(embed_half, "mp", axis=0, tiled=True)
    prototype_logits = jnp.einsum(
        "bvp,kp->bvk", all_embed, proto_half, preferred_element_type=jnp.float32
    )
    transport = jnp.exp(prototype_logits * (1.0 / EPSILON_CODES))
    softmax_exponent = jnp.exp(prototype_logits * (1.0 / SOFTMAX_TEMPER))
    soft_part = jnp.sum(softmax_exponent, axis=-1)
    for iteration in range(ITERS - 1):
        transport = transport / prototype_totals(transport)[None]
        transport = transport / code_totals(transport)[..., None]
    transport = transport / prototype_totals(transport)[None]
    softmax_denominator = lax.psum(soft_part, "mp")
    row_sums = code_totals(transport)
    assignments = transport / row_sums[..., None]
    grad_half, loss_portion = loss_pieces(
        prototype_logits, softmax_exponent, softmax_denominator, assignments, gradient_factor
    )
    proto_grad = jnp.einsum("bvk,bvp->kp", grad_half, all_embed, preferred_element_type=jnp.float32)
    proto_grad = lax.psum(proto_grad, "dp")
    grad_unit = lax.psum_scatter(
        jnp.einsum("bvk,kp->bvp", grad_half, proto_half, preferred_element_type=jnp.float32),
        "mp",
        scatter_dimension=0,
        tiled=True,
    )
    weight_part = embed_backward(grad_unit, embed_unit, embed_inverse, own_feats)
    weight_grad, loss_total = lax.psum((weight_part, loss_portion), ("dp", "mp"))
    along_proto = jnp.sum(proto_unit * proto_grad, axis=-1, keepdims=True)
    grad_protos = (proto_grad - proto_unit * along_proto) * proto_inverse
    loss_value = -loss_total / (2.0 * batch_row_count)
    return (grad_protos, weight_grad, loss_value)


def solution(mesh):
    return jax.shard_map(
        body,
        mesh=mesh,
        in_specs=(P("dp", None, None), P(), P("mp", None)),
        out_specs=(P("mp", None), P(), P()),
        check_vma=False,
    )
```

profile of v0, /device:TPU:2, one launch (start us, length us, event | category | flops | bytes accessed | tf_op | source)
XLA Modules:
  0.0 803.6 jit_solution(7048572155357733132)
XLA Ops:
  7.2 0.0 copy-start
  7.2 0.0 all-gather.2.cloned.1.call-start
  7.2 1.4 constant_dynamic-slice_fusion
  8.7 0.0 copy-start.3
  8.7 0.8 copy-done.3
  9.5 0.0 copy-done
  9.5 0.4 multiply_reduce_fusion.1
  9.9 0.7 multiply_convert_fusion.1
  10.6 0.0 all-gather.2.cloned.1.call-update
  10.6 0.0 reduce-scatter.2.cloned.1.call-start
  10.7 1.1 multiply_reduce_fusion.4
  11.8 49.1 %all-gather.2.cloned.1.call-done = bf16[2048,2,256]{0,2,1:T(8,128)(2,1)} async-done(((bf16[256,2,256]{0,2,1:T(8,128)(2,1)}), bf16[2048,2,256]{0,2,1:T(8,128)(2,1)}) %all-gather.2.cloned.1.call-update) | async-done | bytes 2097168 | tf_op jit(solution)/shard_map/all_gather | solution.py:58
  60.9 5.4 fusion.12
  66.3 53.0 %psum.71 = f32[2,375]{1,0:T(2,128)S(1)} all-reduce(f32[2,375]{1,0:T(2,128)S(1)} %get-tuple-element.11), channel_id=1, replica_groups=mesh['dp'=32,'mp'=8] {'dp'}, use_global_device_ids=true, to_apply=%region_5.0 | all-reduce | flops 750 | bytes 6000 | tf_op jit(solution)/shard_map/psum | solution.py:19
  119.3 3.8 exponential_reduce_fusion
  123.2 29.9 %psum.72 = f32[2048,2]{0,1:T(2,128)S(1)} all-reduce(f32[2048,2]{0,1:T(2,128)S(1)} %get-tuple-element.4), channel_id=1, replica_groups=mesh['dp'=32,'mp'=8] {'mp'}, use_global_device_ids=true, to_apply=%region_7.0 | all-reduce | flops 4096 | bytes 32768 | tf_op jit(solution)/shard_map/psum | solution.py:23
  153.0 4.4 fusion.8
  157.5 54.7 %psum.73 = f32[2,375]{1,0:T(2,128)S(1)} all-reduce(f32[2,375]{1,0:T(2,128)S(1)} %fusion.8), channel_id=1, replica_groups=mesh['dp'=32,'mp'=8] {'dp'}, use_global_device_ids=true, to_apply=%region_9.0 | all-reduce | flops 750 | bytes 6000 | tf_op jit(solution)/shard_map/psum | solution.py:19
  212.1 3.7 fusion.9
  215.9 27.0 %psum.74 = f32[2048,2]{0,1:T(2,128)S(1)} all-reduce(f32[2048,2]{0,1:T(2,128)S(1)} %fusion.9), channel_id=1, replica_groups=mesh['dp'=32,'mp'=8] {'mp'}, use_global_device_ids=true, to_apply=%region_11.0 | all-reduce | flops 4096 | bytes 32768 | tf_op jit(solution)/shard_map/psum | solution.py:23
  242.9 3.9 fusion.10
  246.8 62.7 %psum.75 = f32[2,375]{1,0:T(2,128)S(1)} all-reduce(f32[2,375]{1,0:T(2,128)S(1)} %fusion.10), channel_id=1, replica_groups=mesh['dp'=32,'mp'=8] {'dp'}, use_global_device_ids=true, to_apply=%region_13.0 | all-reduce | flops 750 | bytes 6000 | tf_op jit(solution)/shard_map/psum | solution.py:19
  309.5 4.3 fusion.11
  313.8 27.7 %all-reduce = (f32[2048,2]{0,1:T(2,128)S(1)}, f32[2048,2]{0,1:T(2,128)S(1)}) all-reduce(f32[2048,2]{0,1:T(2,128)S(1)} %fusion.11, f32[2048,2]{0,1:T(2,128)S(1)} %get-tuple-element.3), channel_id=1, replica_groups=mesh['dp'=32,'mp'=8] {'mp'}, use_global_device_ids=true, to_apply=%region_15.0 | all-reduce | flops 8192 | bytes 65536 | tf_op jit(solution)/shard_map/psum | solution.py:23
  341.5 0.0 slice-start.1
  341.5 5.1 fusion.7
  346.6 0.0 slice-done
  346.6 0.0 slice-done.1
  346.7 0.0 copy-start.2
  346.7 2.6 multiply_reduce_fusion
  349.2 1.6 copy-done.1
  350.9 0.0 copy-done.2
  350.9 3.3 fusion.28
  354.2 0.0 reduce-scatter.2.cloned.1.call-update
  354.2 0.0 all-reduce.4.cloned.1.call-start
  354.3 4.3 convolution_bitcast_fusion.1
  358.6 0.0 all-reduce.4.cloned.1.call-update
  358.7 0.0 all-reduce.6.cloned.1.call-start
  358.7 90.6 %psum.79 = f32[]{:T(128)} all-reduce(f32[]{:T(128)} %get-tuple-element.7), channel_id=1, replica_groups=mesh['dp'=32,'mp'=8] {'dp','mp'}, use_global_device_ids=true, to_apply=%region_22.0 | all-reduce | flops 1 | bytes 8 | tf_op jit(solution)/shard_map/psum | solution.py:84
  449.9 0.0 reduce-scatter.2.cloned.1.call-done
  450.0 0.0 copy-done.4
  450.0 2.5 convolution_bitcast_fusion
  452.5 0.0 all-reduce.6.cloned.1.call-update
  452.5 83.7 %all-reduce.4.cloned.1.call-done = f32[375,256]{1,0:T(8,128)} async-done(((f32[375,256]{1,0:T(8,128)}), f32[375,256]{1,0:T(8,128)}) %all-reduce.4.cloned.1.call-update) | async-done | bytes 384016 | tf_op jit(solution)/shard_map/psum | solution.py:76
  536.2 1.2 multiply_reduce_fusion.3
  537.4 1.9 subtract_multiply_fusion
  539.3 254.8 %all-reduce.6.cloned.1.call-done = f32[512,256]{1,0:T(8,128)} async-done(((f32[512,256]{1,0:T(8,128)}), f32[512,256]{1,0:T(8,128)}) %all-reduce.6.cloned.1.call-update) | async-done | bytes 524304 | tf_op jit(solution)/shard_map/psum | solution.py:84
  794.1 1.9 copy.29
  (7 shorter events, 0.0 us)
Async XLA Ops:
  7.2 2.3 copy-start
  7.2 53.7 %all-gather.2.cloned.1.call-start = ((), (), s32[]{:S(2)}) async-start(), calls=%async_computation.1 | async-start | bytes 2359296 | tf_op jit(solution)/shard_map/all_gather | solution.py:58
  8.7 0.8 copy-start.3
  10.6 439.3 %reduce-scatter.2.cloned.1.call-start = ((), (), s32[]{:S(2)}) async-start(), calls=%async_computation.3 | async-start | bytes 4718592 | tf_op jit(solution)/shard_map/reduce_scatter | solution.py:77
  309.5 37.1 %slice-start = ((s8[6160384]{0:T(1024)(128)(4,1)}), s8[1966080]{0:T(1024)(128)(4,1)S(1)}, s32[]{:S(2)}) async-start(s8[6160384]{0:T(1024)(128)(4,1)} %bitcast.19), calls=%async_computation.5 | async-start | bytes 3932160
  341.5 5.1 slice-start.1
  346.7 4.2 copy-start.2
  349.2 1.6 copy-start.1
  354.2 95.8 %copy-start.4 = (bf16[256,2,512]{2,1,0:T(2,128)(2,1)S(1)}, bf16[256,2,512]{2,1,0:T(2,128)(2,1)}, u32[]{:S(2)}) copy-start(bf16[256,2,512]{2,1,0:T(2,128)(2,1)} %copy-done.3) | copy-start | bytes 1572868
  354.2 181.9 %all-reduce.4.cloned.1.call-start = ((), (), s32[]{:S(2)}) async-start(), calls=%async_computation.2 | async-start | bytes 770048 | tf_op jit(solution)/shard_map/psum | solution.py:76
  358.7 435.4 %all-reduce.6.cloned.1.call-start = ((), (), s32[]{:S(2)}) async-start(), calls=%async_computation.4 | async-start | bytes 1048576 | tf_op jit(solution)/shard_map/psum | solution.py:84
Sparse Core Ops, SparseCore 0:
  10.7 50.1 all-gather.1
  354.4 66.9 reduce-scatter.1
  425.2 110.8 all-reduce.3
  542.1 251.9 all-reduce.5
where the time goes:
time: 804 us
  waiting for transfers between devices  388 us (48%)
  blocking collectives  345 us (43%)
  other arithmetic  32.9 us (4%)
  matrix products  16 us (2%)
  between operations  15.7 us (2%)
    psum x1, waiting for transfers between devices, body(): lax.psum((weight_part, loss_portion), ('dp', 'mp'))  255 us
    psum x3, blocking collectives, prototype_totals(): return lax.psum(jnp.sum(values, axis=0), 'dp')  170 us
    psum x1, blocking collectives, body(): lax.psum((weight_part, loss_portion), ('dp', 'mp'))  90.6 us
    psum x3, blocking collectives, code_totals(): return lax.psum(jnp.sum(values, axis=-1), 'mp')  84.6 us
    psum x1, waiting for transfers between devices, body(): proto_grad = lax.psum(proto_grad, 'dp')  83.7 us
    all_gather x1, waiting for transfers between devices, body(): all_embed = lax.all_gather(embed_half, 'mp', axis=0, tiled=True)  49.1 us
  transfers between devices with their start and end apart: 4, of which 3 were waited for; matrix products, arithmetic and copies ran while one was open for 1% of the time, Pallas kernels for 0%

commit v1 on v0

--- a/solution.py
+++ b/solution.py
@@ -55,7 +55,9 @@
     raw_embed = jnp.einsum("bve,ep->bvp", own_feats, projection, preferred_element_type=jnp.float32)
     embed_unit, embed_inverse = unit_rows(raw_embed)
     embed_half = embed_unit.astype(jnp.bfloat16)
-    all_embed = lax.all_gather(embed_half, "mp", axis=0, tiled=True)
+    all_embed = jnp.concatenate(
+        lax.all_to_all(jnp.stack([embed_half] * lax.axis_size("mp")), "mp", 0, 0), axis=0
+    )
     prototype_logits = jnp.einsum(
         "bvp,kp->bvk", all_embed, proto_half, preferred_element_type=jnp.float32
     )

time: 804 us -> 763 us (0.949)
  waiting for transfers between devices: 388 us -> 335 us
  starting transfers between devices: 0.16 us -> 8.59 us
    psum x1, waiting for transfers between devices: 83.7 us -> 29.8 us  [body(): proto_grad = lax.psum(proto_grad, 'dp')]
    all_to_all x0 -> x1, waiting for transfers between devices: none -> 51 us  [body(): lax.all_to_all(jnp.stack([embed_half] * lax.axis_size('mp')), 'mp', 0, 0)]
    all_gather x1 -> x0, waiting for transfers between devices: 49.1 us -> none  [body(): all_embed = lax.all_gather(embed_half, 'mp', axis=0, tiled=True)]
    all_to_all x0 -> x1, starting transfers between devices: none -> 8.46 us  [body(): lax.all_to_all(jnp.stack([embed_half] * lax.axis_size('mp')), 'mp', 0, 0)]
where the time goes in v1:
time: 763 us; the launch traced here: 762 us
  blocking collectives  347 us (45%)
  waiting for transfers between devices  335 us (44%)
  other arithmetic  31.5 us (4%)
  between operations  17.4 us (2%)
  matrix products  13.7 us (2%)
  local copies, waits for them, and re-layouts  9 us (1%)
  starting transfers between devices  8.59 us (1%)
    psum x1, waiting for transfers between devices, body(): lax.psum((weight_part, loss_portion), ('dp', 'mp'))  254 us
    psum x3, blocking collectives, prototype_totals(): return lax.psum(jnp.sum(values, axis=0), 'dp')  173 us
    psum x1, blocking collectives, body(): lax.psum((weight_part, loss_portion), ('dp', 'mp'))  91.2 us
    psum x3, blocking collectives, code_totals(): return lax.psum(jnp.sum(values, axis=-1), 'mp')  83.4 us
    all_to_all x1, waiting for transfers between devices, body(): lax.all_to_all(jnp.stack([embed_half] * lax.axis_size('mp')), 'mp', 0, 0)  51 us
    psum x1, waiting for transfers between devices, body(): proto_grad = lax.psum(proto_grad, 'dp')  29.8 us
  transfers between devices with their start and end apart: 4, of which 3 were waited for; matrix products, arithmetic and copies ran while one was open for 1% of the time, Pallas kernels for 0%

profile of v1, /device:TPU:2, one launch (start us, length us, event | category | flops | bytes accessed | tf_op | source)
XLA Modules:
  0.0 762.3 jit_solution(14065735646661791606)
XLA Ops:
  8.0 0.0 copy-start
  8.0 0.0 copy-start.2
  8.0 1.5 constant_dynamic-slice_fusion
  9.5 0.0 copy-start.5
  9.5 0.8 copy-done.5
  10.3 0.0 copy-done
  10.3 0.4 multiply_reduce_fusion.1
  10.7 0.1 copy.14
  10.9 1.6 stack.2
  12.4 8.5 %all-to-all-start = ((bf16[8,256,2,256]{3,1,2,0:T(8,128)(2,1)}), bf16[8,256,2,256]{3,1,2,0:T(8,128)(2,1)S(1)}, u32[]{:S(2)}, u32[]{:S(2)}) async-start(bf16[8,256,2,256]{3,1,2,0:T(8,128)(2,1)} %stack.2), calls=%async_computation | async-start | bytes 4194304 | tf_op jit(solution)/shard_map/all_to_all | solution.py:59
  20.9 0.0 reduce-scatter.2.cloned.1.call-start
  20.9 0.1 multiply_reduce_fusion.4
  21.1 51.0 %all-to-all-done = bf16[8,256,2,256]{3,1,2,0:T(8,128)(2,1)S(1)} async-done(((bf16[8,256,2,256]{3,1,2,0:T(8,128)(2,1)}), bf16[8,256,2,256]{3,1,2,0:T(8,128)(2,1)S(1)}, u32[]{:S(2)}, u32[]{:S(2)}) %all-to-all-start) | async-done | bytes 2097184 | tf_op jit(solution)/shard_map/all_to_all | solution.py:59
  72.1 0.1 copy.15
  72.2 0.0 copy-start.3
  72.2 1.4 copy-done.3
  73.6 3.7 fusion.12
  77.3 53.0 %psum.71 = f32[2,375]{1,0:T(2,128)S(1)} all-reduce(f32[2,375]{1,0:T(2,128)S(1)} %get-tuple-element.11), channel_id=1, replica_groups=mesh['dp'=32,'mp'=8] {'dp'}, use_global_device_ids=true, to_apply=%region_5.0 | all-reduce | flops 750 | bytes 6000 | tf_op jit(solution)/shard_map/psum | solution.py:19
  130.3 3.8 exponential_reduce_fusion
  134.1 28.7 %psum.72 = f32[2048,2]{0,1:T(2,128)S(1)} all-reduce(f32[2048,2]{0,1:T(2,128)S(1)} %get-tuple-element.4), channel_id=1, replica_groups=mesh['dp'=32,'mp'=8] {'mp'}, use_global_device_ids=true, to_apply=%region_7.0 | all-reduce | flops 4096 | bytes 32768 | tf_op jit(solution)/shard_map/psum | solution.py:23
  162.8 4.5 fusion.8
  167.3 56.9 %psum.73 = f32[2,375]{1,0:T(2,128)S(1)} all-reduce(f32[2,375]{1,0:T(2,128)S(1)} %fusion.8), channel_id=1, replica_groups=mesh['dp'=32,'mp'=8] {'dp'}, use_global_device_ids=true, to_apply=%region_9.0 | all-reduce | flops 750 | bytes 6000 | tf_op jit(solution)/shard_map/psum | solution.py:19
  224.2 3.8 fusion.9
  227.9 27.0 %psum.74 = f32[2048,2]{0,1:T(2,128)S(1)} all-reduce(f32[2048,2]{0,1:T(2,128)S(1)} %fusion.9), channel_id=1, replica_groups=mesh['dp'=32,'mp'=8] {'mp'}, use_global_device_ids=true, to_apply=%region_11.0 | all-reduce | flops 4096 | bytes 32768 | tf_op jit(solution)/shard_map/psum | solution.py:23
  255.0 3.9 fusion.10
  258.9 62.7 %psum.75 = f32[2,375]{1,0:T(2,128)S(1)} all-reduce(f32[2,375]{1,0:T(2,128)S(1)} %fusion.10), channel_id=1, replica_groups=mesh['dp'=32,'mp'=8] {'dp'}, use_global_device_ids=true, to_apply=%region_13.0 | all-reduce | flops 750 | bytes 6000 | tf_op jit(solution)/shard_map/psum | solution.py:19
  321.6 4.4 fusion.11
  326.0 27.7 %all-reduce = (f32[2048,2]{0,1:T(2,128)S(1)}, f32[2048,2]{0,1:T(2,128)S(1)}) all-reduce(f32[2048,2]{0,1:T(2,128)S(1)} %fusion.11, f32[2048,2]{0,1:T(2,128)S(1)} %get-tuple-element.3), channel_id=1, replica_groups=mesh['dp'=32,'mp'=8] {'mp'}, use_global_device_ids=true, to_apply=%region_15.0 | all-reduce | flops 8192 | bytes 65536 | tf_op jit(solution)/shard_map/psum | solution.py:23
  353.7 0.0 slice-start.1
  353.7 5.1 fusion.7
  358.8 2.6 multiply_reduce_fusion
  361.5 1.6 copy-done.1
  363.1 3.3 fusion.28
  366.5 0.0 reduce-scatter.2.cloned.1.call-update
  366.5 0.0 all-reduce.4.cloned.1.call-start
  366.5 0.0 copy-done.4
  366.5 3.7 convolution_bitcast_fusion.1
  370.2 0.0 all-reduce.4.cloned.1.call-update
  370.2 0.0 all-reduce.6.cloned.1.call-start
  370.3 91.2 %psum.79 = f32[]{:T(128)} all-reduce(f32[]{:T(128)} %get-tuple-element.7), channel_id=1, replica_groups=mesh['dp'=32,'mp'=8] {'dp','mp'}, use_global_device_ids=true, to_apply=%region_22.0 | all-reduce | flops 1 | bytes 8 | tf_op jit(solution)/shard_map/psum | solution.py:86
  462.1 0.0 reduce-scatter.2.cloned.1.call-done
  462.1 2.6 convolution_bitcast_fusion
  464.8 0.0 all-reduce.6.cloned.1.call-update
  464.8 29.8 %all-reduce.4.cloned.1.call-done = f32[375,256]{1,0:T(8,128)} async-done(((f32[375,256]{1,0:T(8,128)}), f32[375,256]{1,0:T(8,128)}) %all-reduce.4.cloned.1.call-update) | async-done | bytes 384016 | tf_op jit(solution)/shard_map/psum | solution.py:78
  494.7 1.2 multiply_reduce_fusion.3
  495.9 1.9 subtract_multiply_fusion
  497.8 254.1 %all-reduce.6.cloned.1.call-done = f32[512,256]{1,0:T(8,128)} async-done(((f32[512,256]{1,0:T(8,128)}), f32[512,256]{1,0:T(8,128)}) %all-reduce.6.cloned.1.call-update) | async-done | bytes 524304 | tf_op jit(solution)/shard_map/psum | solution.py:86
  751.9 1.9 copy.33
  (11 shorter events, 0.1 us)
Async XLA Ops:
  8.0 2.3 copy-start
  8.0 12.9 %copy-start.2 = (f32[375,256]{1,0:T(8,128)S(1)}, f32[375,256]{1,0:T(8,128)}, u32[]{:S(2)}) copy-start(f32[375,256]{1,0:T(8,128)} %param.5) | copy-start | bytes 1152004
  9.5 0.8 copy-start.5
  12.4 59.7 %all-to-all-start = ((bf16[8,256,2,256]{3,1,2,0:T(8,128)(2,1)}), bf16[8,256,2,256]{3,1,2,0:T(8,128)(2,1)S(1)}, u32[]{:S(2)}, u32[]{:S(2)}) async-start(bf16[8,256,2,256]{3,1,2,0:T(8,128)(2,1)} %stack.2), calls=%async_computation | async-start | bytes 4194304 | tf_op jit(solution)/shard_map/all_to_all | solution.py:59
  20.9 441.3 %reduce-scatter.2.cloned.1.call-start = ((), (), s32[]{:S(2)}) async-start(), calls=%async_computation.3 | async-start | bytes 4718592 | tf_op jit(solution)/shard_map/reduce_scatter | solution.py:79
  72.2 1.4 copy-start.3
  321.6 37.2 %slice-start = ((s8[6160384]{0:T(1024)(128)(4,1)}), s8[1966080]{0:T(1024)(128)(4,1)S(1)}, s32[]{:S(2)}) async-start(s8[6160384]{0:T(1024)(128)(4,1)} %bitcast.20), calls=%async_computation.5 | async-start | bytes 3932160
  353.7 5.2 slice-start.1
  361.5 1.6 copy-start.1
  361.5 5.1 copy-start.4
  366.5 128.2 %all-reduce.4.cloned.1.call-start = ((), (), s32[]{:S(2)}) async-start(), calls=%async_computation.2 | async-start | bytes 770048 | tf_op jit(solution)/shard_map/psum | solution.py:78
  370.2 381.7 %all-reduce.6.cloned.1.call-start = ((), (), s32[]{:S(2)}) async-start(), calls=%async_computation.4 | async-start | bytes 1048576 | tf_op jit(solution)/shard_map/psum | solution.py:86
Sparse Core Ops, SparseCore 0:
  366.6 66.9 reduce-scatter.1
Sparse Core Ops, SparseCore 1:
  370.8 123.8 all-reduce.3
  500.0 251.8 all-reduce.5
